TPU v7x, 32 devices: a whole 2x2x4 slice. The times are simulated.
32 devices in a mesh: grp: 2 (over x), view: 16 (over z, y, core).
Axes of the slice: x: 2, y: 2, z: 4, core: 2. Of those that a mesh axis runs over, the one named last changes fastest.
Arguments:
- features: float32 [32, 32, 8, 256], P(('grp', 'view')), parts along dimension 0, may hold values from -96 to 96, as said below
- offsets: int32 [32, 128], P(('grp', 'view')), parts along dimension 0, may hold values from 0 to 31
- conf_bins: int32 [16, 256], P('grp'), parts along dimension 0, may hold values from 0 to 3
- plane_depths: float32 [128], P('view'), may hold values from 1 to 10
Outputs:
- cost_volume: float32 [128, 16, 256], P('view', 'grp'), parts along dimension 1
- depth_map: float32 [16, 256], P('grp'), parts along dimension 0
There are 2 independent parts, one for each index of `grp`. A program takes and returns all parts, laid end to end along the dimension named above; an argument that names none is the same for every part. Nothing has to cross between parts.
Inputs may be any that keep to these rules, and one draw needn't show every extreme that they name: `features`: feature entries may be large on some rows.
All inputs are finite; a program needn't handle non-finite values.
Results may differ from a plain program's by a relative error of at most 0.0003.
Values sent between devices are 32-bit elements; how exact they have to be, the bound alone decides.
A program may use at most 128 MiB of HBM per device.

v0:
```python
import functools

import jax
import jax.numpy as jnp
from jax import lax
from jax.experimental import pallas as pl
from jax.experimental.pallas import tpu as pltpu
from jax.sharding import PartitionSpec as P

ITERS = 4
LANES = 128
GROUP = 8


def shifted(x, amount, lane):
    if amount == 0:
        return x
    return jnp.where(lane >= amount, pltpu.roll(x, amount, 1), 0.0)


def kernel(
    n, feat_ref, off_ref, conf_ref, depth_ref, cost_ref, map_ref,
    feat, xs, xr, offv, offs, table, sqs, spad, part, costs, stat_s, stat_r, res,
    local_sem, xs_send, xs_recv, off_send, off_recv, c_send, c_recv, s_send, s_recv, r_send, r_recv,
):
    _, chans, rows, width = feat_ref.shape
    planes = off_ref.shape[-1]
    owned = depth_ref.shape[0]
    groups = n // rows
    cg = chans // groups
    pad = width // 8
    halo = ITERS
    span = 2 * GROUP
    per_window = GROUP // owned
    windows = planes // GROUP
    blocks = windows + 1
    owners, _, share = stat_s.shape
    parts = width // share
    first_owner = (n - owners) // 2
    me = lax.axis_index("view")
    my_window = me // per_window
    near = max(1, 4 // per_window)
    last_window = my_window // near * near + near - 1

    barrier = pltpu.get_barrier_semaphore()

    def greet(k, carry):
        pl.semaphore_signal(barrier, inc=1, device_id={"view": lax.rem(me + k, n)})
        return carry

    lax.fori_loop(1, n, greet, 0)
    fetch = pltpu.make_async_copy(feat_ref.at[0], feat, local_sem)
    fetch.start()
    offv[me] = off_ref[...]
    fetch.wait()
    for r in range(rows):
        line = feat[:, r, :]
        for g in range(groups):
            xs[r * groups + g] = line[g * cg:(g + 1) * cg]
    pl.semaphore_wait(barrier, n - 1)

    def off_copy(slot, peer):
        return pltpu.make_async_remote_copy(
            src_ref=offv.at[slot], dst_ref=offv.at[slot], send_sem=off_send.at[peer],
            recv_sem=off_recv.at[slot], device_id={"view": peer})

    def feat_copy(slot, peer):
        return pltpu.make_async_remote_copy(
            src_ref=xs.at[peer], dst_ref=xr.at[slot], send_sem=xs_send.at[peer],
            recv_sem=xs_recv.at[slot], device_id={"view": peer})

    def send_feat(k, carry):
        peer = lax.rem(me + k, n)
        off_copy(me, peer).start()
        feat_copy(me, peer).start()
        return carry

    lax.fori_loop(1, n, send_feat, 0)

    lane = lax.broadcasted_iota(jnp.int32, (cg, width), 1)

    def build(view, x):
        for o in range(pad):
            table[view * pad + o] = shifted(x, o, lane)
        sqs[pl.ds(view, 1), :] = jnp.sum(x * x, axis=0, keepdims=True)

    build(me, xs[me])

    def receive(k, carry):
        source = lax.rem(me - k + n, n)
        feat_copy(source, source).wait_recv()
        off_copy(source, source).wait_recv()
        build(source, xr[source])
        return carry

    lax.fori_loop(1, n, receive, 0)

    to_scalar = pltpu.make_async_copy(offv, offs, local_sem)
    to_scalar.start()
    chosen = offv[:, 0, :]
    sq = sqs[...]
    lane_n = lax.broadcasted_iota(jnp.int32, (n, width), 1)
    hot = jnp.concatenate(
        [jnp.where(chosen == o, 1.0, 0.0) for o in range(pad)], axis=0)
    sq_all = jnp.concatenate([shifted(sq, o, lane_n) for o in range(pad)], axis=0)
    hot = hot.T.astype(jnp.bfloat16)
    high = sq_all.astype(jnp.bfloat16)
    rest = sq_all - high.astype(jnp.float32)
    mid = rest.astype(jnp.bfloat16)
    low = (rest - mid.astype(jnp.float32)).astype(jnp.bfloat16)
    square = jnp.zeros((planes, width), jnp.float32)
    for piece in (low, mid, high):
        square = square + jnp.dot(hot, piece, preferred_element_type=jnp.float32)
    spad[...] = jnp.zeros_like(spad)
    spad[halo:halo + planes, :] = square * (1.0 / (n * chans))
    to_scalar.wait()

    def cost_copy(slot, peer, window):
        first = pl.multiple_of(window * GROUP, GROUP)
        return pltpu.make_async_remote_copy(
            src_ref=part.at[pl.ds(first, span)], dst_ref=costs.at[slot],
            send_sem=c_send.at[peer], recv_sem=c_recv.at[slot], device_id={"view": peer})

    def send_cost(window):
        for m in range(per_window):
            peer = window * per_window + m

            @pl.when(peer != me)
            def _():
                cost_copy(me, peer, window).start()

    def block(k, carry):
        j = lax.rem(last_window + 1 + k, blocks)
        sums = []
        for i in range(GROUP):
            p = jnp.clip(j * GROUP + i - halo, 0, planes - 1)
            total = table[offs[0, 0, p]]
            for v in range(1, n):
                total = total + table[v * pad + offs[v, 0, p]]
            sums.append(jnp.sum(total * total, axis=0, keepdims=True))
        first = pl.multiple_of(j * GROUP, GROUP)
        part[pl.ds(first, GROUP), :] = (
            spad[pl.ds(first, GROUP), :]
            - jnp.concatenate(sums, axis=0) * (1.0 / (n * n * chans)))

        @pl.when(jnp.logical_and(k > 0, j > 0))
        def _():
            send_cost(j - 1)

        return carry

    lax.fori_loop(0, blocks, block, 0)
    send_cost(last_window)
    costs[me] = part[pl.ds(pl.multiple_of(my_window * GROUP, GROUP), span), :]

    def take(k, carry):
        source = lax.rem(me - k + n, n)
        cost_copy(source, source, 0).wait_recv()
        return carry

    lax.fori_loop(1, n, take, 0)

    plane = my_window * GROUP - halo + lax.broadcasted_iota(jnp.int32, (span, width), 0)
    valid = jnp.logical_and(plane >= 0, plane < planes)
    col = lax.broadcasted_iota(jnp.int32, (span, width), 1)
    cost, rate = [], []
    for r in range(rows):
        total = costs[r * groups]
        for g in range(1, groups):
            total = total + costs[r * groups + g]
        cost.append(jnp.where(valid, total, 0.0))
        conf = (conf_ref[r:r + 1, :].astype(jnp.float32) + 1.0) * 0.25
        rate.append(jnp.where(valid, 0.15 * conf, 0.0))
    for step in range(ITERS):
        new = []
        for r in range(rows):
            c = cost[r]
            beside = pltpu.roll(c, 1, 0) + pltpu.roll(c, span - 1, 0)
            if r > 0:
                beside = beside + cost[r - 1]
            if r < rows - 1:
                beside = beside + cost[r + 1]
            beside = beside + jnp.where(col > 0, pltpu.roll(c, 1, 1), 0.0)
            beside = beside + jnp.where(col < width - 1, pltpu.roll(c, width - 1, 1), 0.0)
            new.append(c + rate[r] * (beside - 6.0 * c))
        cost = new

    index = lax.broadcasted_iota(jnp.int32, (owned, width), 0)
    depth = jnp.zeros((owned, width), jnp.float32)
    for i in range(owned):
        depth = jnp.where(index == i, depth_ref[i], depth)
    for r in range(rows):
        own = cost[r][halo:halo + owned]
        for m in range(1, per_window):
            first = halo + m * owned
            own = jnp.where(lax.rem(me, per_window) == m, cost[r][first:first + owned], own)
        cost_ref[:, r, :] = own
        peak = jnp.max(-own, axis=0, keepdims=True)
        weight = jnp.exp(-own - peak)
        soft = jnp.concatenate(
            [peak, jnp.sum(weight, axis=0, keepdims=True),
             jnp.sum(weight * depth, axis=0, keepdims=True)], axis=0)
        for h in range(parts):
            stat_s[r * parts + h] = soft[:, h * share:(h + 1) * share]

    mine = me - first_owner
    is_owner = jnp.logical_and(mine >= 0, mine < owners)

    def stat_copy(slot, owner):
        return pltpu.make_async_remote_copy(
            src_ref=stat_s.at[owner], dst_ref=stat_r.at[slot], send_sem=s_send.at[owner],
            recv_sem=s_recv.at[slot], device_id={"view": owner + first_owner})

    def res_copy(owner, peer):
        return pltpu.make_async_remote_copy(
            src_ref=res.at[owner], dst_ref=res.at[owner], send_sem=r_send.at[peer],
            recv_sem=r_recv.at[owner], device_id={"view": peer})

    def send_stat(k, carry):
        owner = lax.rem(me + k, owners)

        @pl.when(owner != mine)
        def _():
            stat_copy(me, owner).start()

        return carry

    lax.fori_loop(0, owners, send_stat, 0)

    @pl.when(is_owner)
    def _():
        stat_r[me] = stat_s[mine]

        def wait_stat(k, carry):
            stat_copy(lax.rem(me - k + n, n), mine).wait_recv()
            return carry

        lax.fori_loop(1, n, wait_stat, 0)
        got = stat_r[...]
        top = jnp.max(got[:, 0, :], axis=0, keepdims=True)
        scale = jnp.exp(got[:, 0, :] - top)
        denom = jnp.sum(got[:, 1, :] * scale, axis=0, keepdims=True)
        numer = jnp.sum(got[:, 2, :] * scale, axis=0, keepdims=True)
        res[mine] = numer / denom

        def send_res(k, carry):
            res_copy(mine, lax.rem(me + k, n)).start()
            return carry

        lax.fori_loop(1, n, send_res, 0)

    def finish(k, carry):
        peer = lax.rem(me + k, n)
        feat_copy(me, peer).wait_send()
        off_copy(me, peer).wait_send()
        cost_copy(me, peer, 0).wait_send()

        @pl.when(is_owner)
        def _():
            res_copy(mine, peer).wait_send()

        return carry

    lax.fori_loop(1, n, finish, 0)

    def collect(owner, carry):
        @pl.when(owner != mine)
        def _():
            stat_copy(me, owner).wait_send()
            res_copy(owner, owner + first_owner).wait_recv()

        return carry

    lax.fori_loop(0, owners, collect, 0)
    for r in range(rows):
        for h in range(parts):
            map_ref[r:r + 1, h * share:(h + 1) * share] = res[r * parts + h]


def hand_on(cost_in, map_in, cost_out, map_out):
    cost_out[...] = cost_in[...]
    map_out[...] = map_in[...]


def per_device(features, offsets, conf_bins, plane_depths):
    n = lax.axis_size("view")
    _, chans, rows, width = features.shape
    planes = offsets.shape[-1]
    owned = plane_depths.shape[0]
    cg = chans * rows // n
    pad = width // 8
    chunks = rows * width // LANES
    share = min(max(1, chunks // max(1, n // 2)) * LANES, width)
    owners = rows * width // share
    padded = planes + 2 * ITERS
    f32 = jnp.float32
    vmem = pl.BlockSpec(memory_space=pltpu.VMEM)
    dma = pltpu.SemaphoreType.DMA
    outputs = pl.pallas_call(
        functools.partial(kernel, n),
        out_shape=(
            jax.ShapeDtypeStruct((owned, rows, width), f32),
            jax.ShapeDtypeStruct((rows, width), f32),
        ),
        in_specs=[pl.BlockSpec(memory_space=pl.ANY), vmem, vmem, pl.BlockSpec(memory_space=pltpu.SMEM)],
        out_specs=(vmem, vmem),
        scratch_shapes=[
            pltpu.VMEM((chans, rows, width), f32),
            pltpu.VMEM((n, cg, width), f32),
            pltpu.VMEM((n, cg, width), f32),
            pltpu.VMEM((n, 1, planes), jnp.int32),
            pltpu.SMEM((n, 1, planes), jnp.int32),
            pltpu.VMEM((n * pad, cg, width), f32),
            pltpu.VMEM((n, width), f32),
            pltpu.VMEM((padded, width), f32),
            pltpu.VMEM((padded, width), f32),
            pltpu.VMEM((n, 2 * GROUP, width), f32),
            pltpu.VMEM((owners, 3, share), f32),
            pltpu.VMEM((n, 3, share), f32),
            pltpu.VMEM((owners, 1, share), f32),
            dma,
        ] + [dma((n,)) for _ in range(10)],
        compiler_params=pltpu.CompilerParams(collective_id=0, has_side_effects=True,
                                             vmem_limit_bytes=60 << 20),
    )(features, offsets, conf_bins, plane_depths)
    return pl.pallas_call(
        hand_on,
        out_shape=tuple(jax.ShapeDtypeStruct(x.shape, x.dtype) for x in outputs),
        in_specs=[vmem, vmem],
        out_specs=(vmem, vmem),
    )(*outputs)


def solution(mesh):
    in_specs = (
        P(("grp", "view"), None, None, None),
        P(("grp", "view"), None),
        P("grp", None),
        P("view"),
    )
    out_specs = (P("view", "grp", None), P("grp", None))
    return jax.shard_map(
        per_device, mesh=mesh, in_specs=in_specs, out_specs=out_specs, check_vma=False
    )
```

profile of v0, /device:TPU:0, one launch (start us, length us, event | category | flops | bytes accessed | tf_op | source)
XLA Modules:
  0.0 36.1 jit_solution(15703117118849899863)
XLA Ops:
  0.6 34.0 %shard_map.59 = (f32[8,8,256]{2,1,0:T(8,128)}, f32[8,256]{1,0:T(8,128)}) custom-call(f32[1,32,8,256]{3,2,1,0:T(8,128)} %feat_ref.1, s32[1,128]{1,0:T(1,128)} %off_ref.1, s32[8,256]{1,0:T(8,128)} %conf_ref.1, f32[8]{0:T(128)} %depth_ref.1), custom_call_target="tpu_custom_call" | custom-call | tf_op jit(solution)/shard_map/pallas_call | solution.py:299
  34.6 1.5 %shard_map.60 = (f32[8,8,256]{2,1,0:T(8,128)}, f32[8,256]{1,0:T(8,128)}) custom-call(f32[8,8,256]{2,1,0:T(8,128)} %get-tuple-element.4.cost_in, f32[8,256]{1,0:T(8,128)} %get-tuple-element.5.map_in), custom_call_target="tpu_custom_call" | custom-call | tf_op jit(solution)/shard_map/pallas_call | solution.py:326
where the time goes:
time: 36.4 us; the launch traced here: 36.1 us
  Pallas kernels  35.5 us (98%)
  between operations  0.64 us (2%)
    pallas_call x1, Pallas kernels, per_device(): pl.pallas_call(functools.partial(kernel, n), out_shape=(jax.ShapeDtypeStr...  34 us
    pallas_call x1, Pallas kernels, per_device(): pl.pallas_call(hand_on, out_shape=tuple((jax.ShapeDtypeStruct(x.shape, x....  1.48 us

commit v1 on v0

v1 whole, which is shorter than its diff:
```python
import functools

import jax
import jax.numpy as jnp
from jax import lax
from jax.experimental import pallas as pl
from jax.experimental.pallas import tpu as pltpu
from jax.sharding import PartitionSpec as P

ITERS = 4
LANES = 128
GROUP = 8


def each(start, end, body):
    if end - start < 16:
        for k in range(start, end):
            body(k)
        return

    def step(k, carry):
        body(k)
        return carry

    lax.fori_loop(start, end, step, 0)


def portions(n):
    ends = [n * part // 16 for part in (5, 10, 14, 16)]
    starts = [0] + ends[:-1]
    return [(a, b) for a, b in zip(starts, ends) if b > a]


def kernel(
    n, feat_ref, off_ref, conf_ref, depth_ref, out_ref,
    feat, xs, xr, aux, deps, offv, offs, table, acc, sqs, picks, hots, part, costq, costs, rateq, rates, depcol, vs,
    local_sem, xs_send, xs_recv, aux_send, aux_recv, d_send, d_recv, c_send, c_recv, v_send, v_recv,
):
    _, chans, rows, width = feat_ref.shape
    planes = off_ref.shape[-1]
    owned = depth_ref.shape[0]
    groups = n // rows
    cg = chans // groups
    pad = width // 8
    halo = ITERS
    pix = width // n
    step = max(GROUP, pix)
    span = step + 2 * halo
    per_window = step // pix
    lanes_out = vs.shape[-1]
    chunks = width // LANES
    entry_rows = chunks * cg
    me = lax.axis_index("view")

    lane = lax.broadcasted_iota(jnp.int32, (cg, LANES), 1)

    def build(place, x):
        pieces = [x[:, c * LANES:(c + 1) * LANES] for c in range(chunks)]
        for o in range(pad):
            turned = [pltpu.roll(piece, o, 1) if o else piece for piece in pieces]
            for c in range(chunks):
                before = turned[c - 1] if c else jnp.zeros_like(turned[c])
                line = jnp.where(lane >= o, turned[c], before) if o else turned[c]
                table[place * pad + o, c * cg:(c + 1) * cg, :] = line
        sqs[pl.ds(place, 1), :] = jnp.sum(x * x, axis=0, keepdims=True)

    barrier = pltpu.get_barrier_semaphore()

    def greet(k, carry):
        pl.semaphore_signal(barrier, inc=1, device_id={"view": lax.rem(me + k, n)})
        return carry

    lax.fori_loop(1, n, greet, 0)
    fetch = pltpu.make_async_copy(feat_ref.at[0], feat, local_sem)
    fetch.start()
    plane_lane = lax.broadcasted_iota(jnp.int32, (1, planes), 1)
    depth_row = jnp.zeros((1, planes), jnp.float32)
    for i in range(owned):
        depth_row = jnp.where(plane_lane == me * owned + i, depth_ref[i], depth_row)
    aux[me] = off_ref[...]
    deps[me] = depth_row
    fetch.wait()
    for r in range(rows):
        line = feat[:, r, :]
        for g in range(groups):
            xs[r * groups + g] = line[g * cg:(g + 1) * cg]
    pl.semaphore_wait(barrier, n - 1)

    def aux_copy(slot, peer):
        return pltpu.make_async_remote_copy(
            src_ref=aux.at[slot], dst_ref=aux.at[slot], send_sem=aux_send.at[peer],
            recv_sem=aux_recv.at[slot], device_id={"view": peer})

    def dep_copy(slot, peer):
        return pltpu.make_async_remote_copy(
            src_ref=deps.at[slot], dst_ref=deps.at[slot], send_sem=d_send.at[peer],
            recv_sem=d_recv.at[slot], device_id={"view": peer})

    def feat_copy(slot, peer):
        return pltpu.make_async_remote_copy(
            src_ref=xs.at[peer], dst_ref=xr.at[slot], send_sem=xs_send.at[peer],
            recv_sem=xs_recv.at[slot], device_id={"view": peer})

    each(1, n, lambda k: aux_copy(me, lax.rem(me + k, n)).start())
    each(1, n, lambda k: feat_copy(me, lax.rem(me + k, n)).start())
    each(1, n, lambda k: dep_copy(me, lax.rem(me + k, n)).start())
    build(0, xs[me])

    conf = (conf_ref[...].astype(jnp.float32) + 1.0) * 0.25
    rate = 0.15 * conf
    rate = jnp.concatenate([rate, jnp.zeros((LANES - rows, width), jnp.float32)], axis=0)
    rateq[...] = jnp.zeros_like(rateq)
    rateq[halo:halo + width, :] = rate.T
    first_pixel = pl.multiple_of(me // per_window * step, GROUP)
    near = rateq[pl.ds(first_pixel, span), :]
    for r in range(rows):
        rates[r] = jnp.broadcast_to(near[:, r:r + 1], (span, planes))
    costq[0:GROUP, :] = jnp.zeros((GROUP, planes), jnp.float32)
    costq[width:width + 2 * halo, :] = jnp.zeros((2 * halo, planes), jnp.float32)
    part[...] = jnp.zeros_like(part)

    shift = lax.broadcasted_iota(jnp.int32, (pad, width), 0)
    inside = lax.broadcasted_iota(jnp.int32, (pad, width), 1) >= shift

    per_hot = LANES // pad

    def squares(h, start, end):
        lines = []
        for k in range(h * per_hot, (h + 1) * per_hot):
            if start <= k < end:
                line = jnp.broadcast_to(sqs[k:k + 1, :], (pad, width))
                line = pltpu.roll(line, 0, 1, stride=1, stride_axis=0)
                lines.append(jnp.where(inside, line, 0.0))
            else:
                lines.append(jnp.zeros((pad, width), jnp.float32))
        sq_all = jnp.concatenate(lines, axis=0)
        high = sq_all.astype(jnp.bfloat16)
        rest = sq_all - high.astype(jnp.float32)
        mid = rest.astype(jnp.bfloat16)
        low = (rest - mid.astype(jnp.float32)).astype(jnp.bfloat16)
        square = jnp.zeros((planes, width), jnp.float32)
        for piece in (low, mid, high):
            square = square + jnp.dot(hots[h], piece, preferred_element_type=jnp.float32)
        part[...] += square * (1.0 / (n * chans))

    def accumulate(start, end, is_last):
        def body(j, carry):
            sums = []
            for i in range(GROUP):
                p = j * GROUP + i
                total = acc[p] if start else None
                for k in range(start, end):
                    entry = table[offs[k, p]]
                    total = entry if total is None else total + entry
                if is_last:
                    total = total * total
                    sums.append(jnp.concatenate(
                        [jnp.sum(total[c * cg:(c + 1) * cg], axis=0, keepdims=True) for c in range(chunks)],
                        axis=1))
                else:
                    acc[p] = total
            if is_last:
                first = pl.multiple_of(j * GROUP, GROUP)
                part[pl.ds(first, GROUP), :] = (
                    part[pl.ds(first, GROUP), :]
                    - jnp.concatenate(sums, axis=0) * (1.0 / (n * n * chans)))
            return carry

        lax.fori_loop(0, planes // GROUP, body, 0)

    def take_offsets():
        each(1, n, lambda k: aux_copy(lax.rem(me - k + n, n), lax.rem(me - k + n, n)).wait_recv())
        for k in range(n):
            picks[k:k + 1, :] = aux[lax.rem(me - k + n, n)]
        places = lax.broadcasted_iota(jnp.int32, (n, planes), 0)
        offv[...] = picks[...] + places * pad
        to_scalar = pltpu.make_async_copy(offv, offs, local_sem)
        to_scalar.start()
        amount = lax.broadcasted_iota(jnp.int32, (pad, planes), 0)
        for h in range(n // per_hot):
            hot = jnp.concatenate(
                [jnp.where(picks[k:k + 1, :] == amount, 1.0, 0.0)
                 for k in range(h * per_hot, (h + 1) * per_hot)], axis=0)
            hots[h] = hot.T.astype(jnp.bfloat16)
        to_scalar.wait()

    for start, end in portions(n):
        first = max(start, 1)

        def receive(k, count):
            sources = [lax.rem(me - k - i + n, n) for i in range(count)]
            for source in sources:
                feat_copy(source, source).wait_recv()
            for i, source in enumerate(sources):
                build(k + i, xr[source])

        def receive_two(i, carry):
            receive(first + 2 * i, 2)
            return carry

        lax.fori_loop(0, (end - first) // 2, receive_two, 0)
        if (end - first) % 2:
            receive(end - 1, 1)
        if start == 0:
            take_offsets()
        for h in range(start // per_hot, (end - 1) // per_hot + 1):
            squares(h, start, end)
        accumulate(start, end, end == n)

    costq[halo:halo + width, :] = part[...].T

    def cost_copy(slot, peer):
        first = pl.multiple_of(peer // per_window * step, GROUP)
        return pltpu.make_async_remote_copy(
            src_ref=costq.at[pl.ds(first, span)], dst_ref=costs.at[slot],
            send_sem=c_send.at[peer], recv_sem=c_recv.at[slot], device_id={"view": peer})

    each(1, n, lambda k: cost_copy(me, lax.rem(me + k, n)).start())
    each(1, n, lambda k: dep_copy(lax.rem(me - k + n, n), lax.rem(me - k + n, n)).wait_recv())
    all_depths = jnp.sum(deps[:, 0, :], axis=0, keepdims=True)
    depcol[...] = jnp.broadcast_to(all_depths, (lanes_out, planes)).T
    costs[me] = costq[pl.ds(first_pixel, span), :]

    each(1, n, lambda k: cost_copy(lax.rem(me - k + n, n), lax.rem(me - k + n, n)).wait_recv())

    plane = lax.broadcasted_iota(jnp.int32, (span, planes), 1)
    cost = []
    for r in range(rows):
        total = costs[r * groups]
        for g in range(1, groups):
            total = total + costs[r * groups + g]
        cost.append(total)
    for _ in range(ITERS):
        new = []
        for r in range(rows):
            c = cost[r]
            beside = pltpu.roll(c, 1, 0) + pltpu.roll(c, span - 1, 0)
            if r > 0:
                beside = beside + cost[r - 1]
            if r < rows - 1:
                beside = beside + cost[r + 1]
            beside = beside + jnp.where(plane > 0, pltpu.roll(c, 1, 1), 0.0)
            beside = beside + jnp.where(plane < planes - 1, pltpu.roll(c, planes - 1, 1), 0.0)
            new.append(c + rates[r] * (beside - 6.0 * c))
        cost = new

    mine = []
    for r in range(rows):
        own = cost[r][halo:halo + pix]
        for m in range(1, per_window):
            first = halo + m * pix
            own = jnp.where(lax.rem(me, per_window) == m, cost[r][first:first + pix], own)
        mine.append(own)
    if lanes_out > rows * pix:
        mine.append(jnp.zeros((lanes_out - rows * pix, planes), jnp.float32))
    final = jnp.concatenate(mine, axis=0).T
    peak = jnp.max(-final, axis=0, keepdims=True)
    weight = jnp.exp(-final - peak)
    denom = jnp.sum(weight, axis=0, keepdims=True)
    numer = jnp.sum(weight * depcol[...], axis=0, keepdims=True)
    depth = numer / denom
    for j in range(n):
        vs[j, 0:owned, :] = final[j * owned:(j + 1) * owned]
        vs[j, owned:owned + 1, :] = depth

    def out_copy(slot, peer):
        return pltpu.make_async_remote_copy(
            src_ref=vs.at[peer], dst_ref=out_ref.at[slot],
            send_sem=v_send.at[peer], recv_sem=v_recv.at[slot], device_id={"view": peer})

    each(1, n, lambda k: out_copy(me, lax.rem(me + k, n)).start())
    out_ref[me] = vs[me]

    def finish(k, carry):
        peer = lax.rem(me + k, n)
        aux_copy(me, peer).wait_send()
        dep_copy(me, peer).wait_send()
        feat_copy(me, peer).wait_send()
        cost_copy(me, peer).wait_send()
        return carry

    lax.fori_loop(1, n, finish, 0)

    each(1, n, lambda k: out_copy(lax.rem(me - k + n, n), lax.rem(me - k + n, n)).wait_recv())
    each(1, n, lambda k: out_copy(me, lax.rem(me + k, n)).wait_send())


def lay_out(pieces, cost_out, map_out):
    n = pieces.shape[0]
    owned, rows, width = cost_out.shape
    pix = width // n
    per_chunk = LANES // pix
    lane = lax.broadcasted_iota(jnp.int32, (owned + 1, LANES), 1) // pix
    for c in range(width // LANES):
        for r in range(rows):
            line = None
            for k in range(per_chunk):
                piece = pieces[c * per_chunk + k]
                shift = (k - r) * pix % LANES
                if shift:
                    piece = pltpu.roll(piece, shift, 1)
                line = piece if line is None else jnp.where(lane == k, piece, line)
            cost_out[:, r, c * LANES:(c + 1) * LANES] = line[:owned]
            map_out[r:r + 1, c * LANES:(c + 1) * LANES] = line[owned:]


def per_device(features, offsets, conf_bins, plane_depths):
    n = lax.axis_size("view")
    _, chans, rows, width = features.shape
    planes = offsets.shape[-1]
    owned = plane_depths.shape[0]
    cg = chans * rows // n
    pad = width // 8
    pix = width // n
    span = max(GROUP, pix) + 2 * ITERS
    lanes_out = max(LANES, rows * pix)
    f32 = jnp.float32
    vmem = pl.BlockSpec(memory_space=pltpu.VMEM)
    dma = pltpu.SemaphoreType.DMA
    pieces = pl.pallas_call(
        functools.partial(kernel, n),
        out_shape=jax.ShapeDtypeStruct((n, owned + 1, lanes_out), f32),
        in_specs=[pl.BlockSpec(memory_space=pl.ANY), vmem, vmem, pl.BlockSpec(memory_space=pltpu.SMEM)],
        out_specs=vmem,
        scratch_shapes=[
            pltpu.VMEM((chans, rows, width), f32),
            pltpu.VMEM((n, cg, width), f32),
            pltpu.VMEM((n, cg, width), f32),
            pltpu.VMEM((n, 1, planes), jnp.int32),
            pltpu.VMEM((n, 1, planes), f32),
            pltpu.VMEM((n, planes), jnp.int32),
            pltpu.SMEM((n, planes), jnp.int32),
            pltpu.VMEM((n * pad, cg * width // LANES, LANES), f32),
            pltpu.VMEM((planes, cg * width // LANES, LANES), f32),
            pltpu.VMEM((n, width), f32),
            pltpu.VMEM((n, planes), jnp.int32),
            pltpu.VMEM((n * pad // LANES, planes, LANES), jnp.bfloat16),
            pltpu.VMEM((planes, width), f32),
            pltpu.VMEM((width + 2 * ITERS, planes), f32),
            pltpu.VMEM((n, span, planes), f32),
            pltpu.VMEM((width + 2 * ITERS, LANES), f32),
            pltpu.VMEM((rows, span, planes), f32),
            pltpu.VMEM((planes, lanes_out), f32),
            pltpu.VMEM((n, owned + 1, lanes_out), f32),
            dma,
        ] + [dma((n,)) for _ in range(10)],
        compiler_params=pltpu.CompilerParams(collective_id=0, has_side_effects=True,
                                             vmem_limit_bytes=60 << 20),
    )(features, offsets, conf_bins, plane_depths)
    return pl.pallas_call(
        lay_out,
        out_shape=(
            jax.ShapeDtypeStruct((owned, rows, width), f32),
            jax.ShapeDtypeStruct((rows, width), f32),
        ),
        in_specs=[vmem],
        out_specs=(vmem, vmem),
    )(pieces)


def solution(mesh):
    in_specs = (
        P(("grp", "view"), None, None, None),
        P(("grp", "view"), None),
        P("grp", None),
        P("view"),
    )
    out_specs = (P("view", "grp", None), P("grp", None))
    return jax.shard_map(
        per_device, mesh=mesh, in_specs=in_specs, out_specs=out_specs, check_vma=False
    )
```

time: 36.4 us -> 34.4 us (0.945)
  Pallas kernels: 35.5 us -> 33.6 us
    pallas_call x2, Pallas kernels: 35.5 us -> 33.6 us  [the longest x1 31.8 us: per_device(): pl.pallas_call(functools.partial(kernel, n), out_shape=jax.ShapeDtypeStru...]
where the time goes in v1:
time: 34.4 us; the launch traced here: 34.2 us
  Pallas kernels  33.6 us (98%)
  between operations  0.64 us (2%)
    pallas_call x1, Pallas kernels, per_device(): pl.pallas_call(functools.partial(kernel, n), out_shape=jax.ShapeDtypeStru...  31.8 us
    pallas_call x1, Pallas kernels, per_device(): pl.pallas_call(lay_out, out_shape=(jax.ShapeDtypeStruct((owned, rows, wid...  1.82 us

profile of v1, /device:TPU:0, one launch (start us, length us, event | category | flops | bytes accessed | tf_op | source)
XLA Modules:
  0.0 34.2 jit_solution(17353697393053940914)
XLA Ops:
  0.6 31.8 %shard_map.59.pieces = f32[16,9,128]{2,1,0:T(8,128)} custom-call(f32[1,32,8,256]{3,2,1,0:T(8,128)} %feat_ref.1, s32[1,128]{1,0:T(1,128)} %off_ref.1, s32[8,256]{1,0:T(8,128)} %conf_ref.1, f32[8]{0:T(128)} %depth_ref.1), custom_call_target="tpu_custom_call" | custom-call | tf_op jit(solution)/shard_map/pallas_call | solution.py:320
  32.4 1.8 %shard_map.60 = (f32[8,8,256]{2,1,0:T(8,128)}, f32[8,256]{1,0:T(8,128)}) custom-call(f32[16,9,128]{2,1,0:T(8,128)} %shard_map.59.pieces), custom_call_target="tpu_custom_call" | custom-call | tf_op jit(solution)/shard_map/pallas_call | solution.py:350

commit v2 on v1

--- a/solution.py
+++ b/solution.py
@@ -26,15 +26,15 @@
 
 
 def portions(n):
-    ends = [n * part // 16 for part in (5, 10, 14, 16)]
+    ends = [n * part // 16 for part in (5, 12, 16)]
     starts = [0] + ends[:-1]
     return [(a, b) for a, b in zip(starts, ends) if b > a]
 
 
 def kernel(
     n, feat_ref, off_ref, conf_ref, depth_ref, out_ref,
-    feat, xs, xr, aux, deps, offv, offs, table, acc, sqs, picks, hots, part, costq, costs, rateq, rates, depcol, vs,
-    local_sem, xs_send, xs_recv, aux_send, aux_recv, d_send, d_recv, c_send, c_recv, v_send, v_recv,
+    feat, xs, xr, aux, deps, offv, offs, table, acc, sqs, picks, hots, part, costq, halves, summed, costs, rateq, rates, depcol, vs,
+    local_sem, xs_send, xs_recv, aux_send, aux_recv, d_send, d_recv, h_send, h_recv, c_send, c_recv, v_send, v_recv,
 ):
     _, chans, rows, width = feat_ref.shape
     planes = off_ref.shape[-1]
@@ -51,6 +51,13 @@
     chunks = width // LANES
     entry_rows = chunks * cg
     me = lax.axis_index("view")
+    my_row, my_group = me // groups, lax.rem(me, groups)
+    reach = halves.shape[1]
+
+    def block_of(device):
+        return lax.rem(device, groups) * rows + device // groups
+
+    my_block = block_of(me)
 
     lane = lax.broadcasted_iota(jnp.int32, (cg, LANES), 1)
 
@@ -111,7 +118,7 @@
     rate = jnp.concatenate([rate, jnp.zeros((LANES - rows, width), jnp.float32)], axis=0)
     rateq[...] = jnp.zeros_like(rateq)
     rateq[halo:halo + width, :] = rate.T
-    first_pixel = pl.multiple_of(me // per_window * step, GROUP)
+    first_pixel = pl.multiple_of(my_block // per_window * step, GROUP)
     near = rateq[pl.ds(first_pixel, span), :]
     for r in range(rows):
         rates[r] = jnp.broadcast_to(near[:, r:r + 1], (span, planes))
@@ -124,15 +131,12 @@
 
     per_hot = LANES // pad
 
-    def squares(h, start, end):
+    def squares(h):
         lines = []
         for k in range(h * per_hot, (h + 1) * per_hot):
-            if start <= k < end:
-                line = jnp.broadcast_to(sqs[k:k + 1, :], (pad, width))
-                line = pltpu.roll(line, 0, 1, stride=1, stride_axis=0)
-                lines.append(jnp.where(inside, line, 0.0))
-            else:
-                lines.append(jnp.zeros((pad, width), jnp.float32))
+            line = jnp.broadcast_to(sqs[k:k + 1, :], (pad, width))
+            line = pltpu.roll(line, 0, 1, stride=1, stride_axis=0)
+            lines.append(jnp.where(inside, line, 0.0))
         sq_all = jnp.concatenate(lines, axis=0)
         high = sq_all.astype(jnp.bfloat16)
         rest = sq_all - high.astype(jnp.float32)
@@ -184,6 +188,7 @@
             hots[h] = hot.T.astype(jnp.bfloat16)
         to_scalar.wait()
 
+    done = 0
     for start, end in portions(n):
         first = max(start, 1)
 
@@ -203,33 +208,49 @@
             receive(end - 1, 1)
         if start == 0:
             take_offsets()
-        for h in range(start // per_hot, (end - 1) // per_hot + 1):
-            squares(h, start, end)
+        while (done + 1) * per_hot <= end:
+            squares(done)
+            done += 1
         accumulate(start, end, end == n)
 
     costq[halo:halo + width, :] = part[...].T
 
-    def cost_copy(slot, peer):
-        first = pl.multiple_of(peer // per_window * step, GROUP)
-        return pltpu.make_async_remote_copy(
-            src_ref=costq.at[pl.ds(first, span)], dst_ref=costs.at[slot],
-            send_sem=c_send.at[peer], recv_sem=c_recv.at[slot], device_id={"view": peer})
-
-    each(1, n, lambda k: cost_copy(me, lax.rem(me + k, n)).start())
+    def reach_of(group):
+        return pl.ds(pl.multiple_of(group * (rows // per_window) * step, GROUP), reach)
+
+    def half_copy(slot, group):
+        return pltpu.make_async_remote_copy(
+            src_ref=costq.at[reach_of(group)], dst_ref=halves.at[slot],
+            send_sem=h_send.at[group], recv_sem=h_recv.at[slot],
+            device_id={"view": my_row * groups + group})
+
+    each(1, groups, lambda k: half_copy(my_group, lax.rem(my_group + k, groups)).start())
+    summed[...] = costq[reach_of(my_group), :]
+
+    def add_half(k):
+        source = lax.rem(my_group - k + groups, groups)
+        half_copy(source, source).wait_recv()
+        summed[...] += halves[source]
+
+    each(1, groups, add_half)
+
+    def cost_copy(slot, row):
+        first = pl.multiple_of(row // per_window * step, GROUP)
+        return pltpu.make_async_remote_copy(
+            src_ref=summed.at[pl.ds(first, span)], dst_ref=costs.at[slot],
+            send_sem=c_send.at[row], recv_sem=c_recv.at[slot],
+            device_id={"view": row * groups + my_group})
+
+    each(1, rows, lambda k: cost_copy(my_row, lax.rem(my_row + k, rows)).start())
     each(1, n, lambda k: dep_copy(lax.rem(me - k + n, n), lax.rem(me - k + n, n)).wait_recv())
     all_depths = jnp.sum(deps[:, 0, :], axis=0, keepdims=True)
     depcol[...] = jnp.broadcast_to(all_depths, (lanes_out, planes)).T
-    costs[me] = costq[pl.ds(first_pixel, span), :]
-
-    each(1, n, lambda k: cost_copy(lax.rem(me - k + n, n), lax.rem(me - k + n, n)).wait_recv())
+    costs[my_row] = summed[pl.ds(pl.multiple_of(my_row // per_window * step, GROUP), span), :]
+
+    each(1, rows, lambda k: cost_copy(lax.rem(my_row - k + rows, rows), lax.rem(my_row - k + rows, rows)).wait_recv())
 
     plane = lax.broadcasted_iota(jnp.int32, (span, planes), 1)
-    cost = []
-    for r in range(rows):
-        total = costs[r * groups]
-        for g in range(1, groups):
-            total = total + costs[r * groups + g]
-        cost.append(total)
+    cost = [costs[r] for r in range(rows)]
     for _ in range(ITERS):
         new = []
         for r in range(rows):
@@ -249,7 +270,7 @@
         own = cost[r][halo:halo + pix]
         for m in range(1, per_window):
             first = halo + m * pix
-            own = jnp.where(lax.rem(me, per_window) == m, cost[r][first:first + pix], own)
+            own = jnp.where(lax.rem(my_block, per_window) == m, cost[r][first:first + pix], own)
         mine.append(own)
     if lanes_out > rows * pix:
         mine.append(jnp.zeros((lanes_out - rows * pix, planes), jnp.float32))
@@ -268,21 +289,22 @@
             src_ref=vs.at[peer], dst_ref=out_ref.at[slot],
             send_sem=v_send.at[peer], recv_sem=v_recv.at[slot], device_id={"view": peer})
 
-    each(1, n, lambda k: out_copy(me, lax.rem(me + k, n)).start())
-    out_ref[me] = vs[me]
+    each(1, n, lambda k: out_copy(my_block, lax.rem(me + k, n)).start())
+    out_ref[my_block] = vs[me]
 
     def finish(k, carry):
         peer = lax.rem(me + k, n)
         aux_copy(me, peer).wait_send()
         dep_copy(me, peer).wait_send()
         feat_copy(me, peer).wait_send()
-        cost_copy(me, peer).wait_send()
         return carry
 
     lax.fori_loop(1, n, finish, 0)
-
-    each(1, n, lambda k: out_copy(lax.rem(me - k + n, n), lax.rem(me - k + n, n)).wait_recv())
-    each(1, n, lambda k: out_copy(me, lax.rem(me + k, n)).wait_send())
+    each(1, groups, lambda k: half_copy(my_group, lax.rem(my_group + k, groups)).wait_send())
+    each(1, rows, lambda k: cost_copy(my_row, lax.rem(my_row + k, rows)).wait_send())
+
+    each(1, n, lambda k: out_copy(block_of(lax.rem(me - k + n, n)), lax.rem(me - k + n, n)).wait_recv())
+    each(1, n, lambda k: out_copy(my_block, lax.rem(me + k, n)).wait_send())
 
 
 def lay_out(pieces, cost_out, map_out):
@@ -312,7 +334,10 @@
     cg = chans * rows // n
     pad = width // 8
     pix = width // n
-    span = max(GROUP, pix) + 2 * ITERS
+    groups = n // rows
+    step = max(GROUP, pix)
+    span = step + 2 * ITERS
+    reach = (rows * pix // step - 1) * step + span
     lanes_out = max(LANES, rows * pix)
     f32 = jnp.float32
     vmem = pl.BlockSpec(memory_space=pltpu.VMEM)
@@ -337,13 +362,15 @@
             pltpu.VMEM((n * pad // LANES, planes, LANES), jnp.bfloat16),
             pltpu.VMEM((planes, width), f32),
             pltpu.VMEM((width + 2 * ITERS, planes), f32),
-            pltpu.VMEM((n, span, planes), f32),
+            pltpu.VMEM((groups, reach, planes), f32),
+            pltpu.VMEM((reach, planes), f32),
+            pltpu.VMEM((rows, span, planes), f32),
             pltpu.VMEM((width + 2 * ITERS, LANES), f32),
             pltpu.VMEM((rows, span, planes), f32),
             pltpu.VMEM((planes, lanes_out), f32),
             pltpu.VMEM((n, owned + 1, lanes_out), f32),
             dma,
-        ] + [dma((n,)) for _ in range(10)],
+        ] + [dma((n,)) for _ in range(6)] + [dma((groups,))] * 2 + [dma((rows,))] * 2 + [dma((n,))] * 2,
         compiler_params=pltpu.CompilerParams(collective_id=0, has_side_effects=True,
                                              vmem_limit_bytes=60 << 20),
     )(features, offsets, conf_bins, plane_depths)

time: 34.4 us -> 33.4 us (0.971)
  Pallas kernels: 33.6 us -> 32.6 us
    pallas_call x1, Pallas kernels: 31.8 us -> 30.7 us  [per_device(): pl.pallas_call(functools.partial(kernel, n), out_shape=jax.ShapeDtypeStru...]
where the time goes in v2:
time: 33.4 us; the launch traced here: 33.2 us
  Pallas kernels  32.6 us (98%)
  between operations  0.64 us (2%)
    pallas_call x1, Pallas kernels, per_device(): pl.pallas_call(functools.partial(kernel, n), out_shape=jax.ShapeDtypeStru...  30.7 us
    pallas_call x1, Pallas kernels, per_device(): pl.pallas_call(lay_out, out_shape=(jax.ShapeDtypeStruct((owned, rows, wid...  1.82 us

profile of v2, /device:TPU:0, one launch (start us, length us, event | category | flops | bytes accessed | tf_op | source)
XLA Modules:
  0.0 33.2 jit_solution(3418448602602163525)
XLA Ops:
  0.6 30.7 %shard_map.59.pieces = f32[16,9,128]{2,1,0:T(8,128)} custom-call(f32[1,32,8,256]{3,2,1,0:T(8,128)} %feat_ref.1, s32[1,128]{1,0:T(1,128)} %off_ref.1, s32[8,256]{1,0:T(8,128)} %conf_ref.1, f32[8]{0:T(128)} %depth_ref.1), custom_call_target="tpu_custom_call" | custom-call | tf_op jit(solution)/shard_map/pallas_call | solution.py:345
  31.4 1.8 %shard_map.60 = (f32[8,8,256]{2,1,0:T(8,128)}, f32[8,256]{1,0:T(8,128)}) custom-call(f32[16,9,128]{2,1,0:T(8,128)} %shard_map.59.pieces), custom_call_target="tpu_custom_call" | custom-call | tf_op jit(solution)/shard_map/pallas_call | solution.py:377

commit v3 on v2

--- a/solution.py
+++ b/solution.py
@@ -26,7 +26,7 @@
 
 
 def portions(n):
-    ends = [n * part // 16 for part in (5, 12, 16)]
+    ends = [n * part // 16 for part in (6, 13, 16)]
     starts = [0] + ends[:-1]
     return [(a, b) for a, b in zip(starts, ends) if b > a]
 
@@ -34,7 +34,7 @@
 def kernel(
     n, feat_ref, off_ref, conf_ref, depth_ref, out_ref,
     feat, xs, xr, aux, deps, offv, offs, table, acc, sqs, picks, hots, part, costq, halves, summed, costs, rateq, rates, depcol, vs,
-    local_sem, xs_send, xs_recv, aux_send, aux_recv, d_send, d_recv, h_send, h_recv, c_send, c_recv, v_send, v_recv,
+    local_sem, o_sem, xs_send, xs_recv, aux_send, aux_recv, d_send, d_recv, h_send, h_recv, c_send, c_recv, v_send, v_recv,
 ):
     _, chans, rows, width = feat_ref.shape
     planes = off_ref.shape[-1]
@@ -68,7 +68,8 @@
             for c in range(chunks):
                 before = turned[c - 1] if c else jnp.zeros_like(turned[c])
                 line = jnp.where(lane >= o, turned[c], before) if o else turned[c]
-                table[place * pad + o, c * cg:(c + 1) * cg, :] = line
+                first = pl.multiple_of(place * pad * entry_rows, GROUP) + o * entry_rows + c * cg
+                table[pl.ds(first, cg), :] = line
         sqs[pl.ds(place, 1), :] = jnp.sum(x * x, axis=0, keepdims=True)
 
     barrier = pltpu.get_barrier_semaphore()
@@ -154,7 +155,7 @@
                 p = j * GROUP + i
                 total = acc[p] if start else None
                 for k in range(start, end):
-                    entry = table[offs[k, p]]
+                    entry = table[pl.ds(offs[k][0, p], entry_rows), :]
                     total = entry if total is None else total + entry
                 if is_last:
                     total = total * total
@@ -170,23 +171,28 @@
                     - jnp.concatenate(sums, axis=0) * (1.0 / (n * n * chans)))
             return carry
 
-        lax.fori_loop(0, planes // GROUP, body, 0)
+        def body_two(j, carry):
+            return body(2 * j + 1, body(2 * j, carry))
+
+        lax.fori_loop(0, planes // GROUP // 2, body_two, 0)
 
     def take_offsets():
         each(1, n, lambda k: aux_copy(lax.rem(me - k + n, n), lax.rem(me - k + n, n)).wait_recv())
         for k in range(n):
             picks[k:k + 1, :] = aux[lax.rem(me - k + n, n)]
         places = lax.broadcasted_iota(jnp.int32, (n, planes), 0)
-        offv[...] = picks[...] + places * pad
-        to_scalar = pltpu.make_async_copy(offv, offs, local_sem)
-        to_scalar.start()
+        offv[:, 0, :] = (picks[...] + places * pad) * entry_rows
+        to_scalar = [pltpu.make_async_copy(offv.at[k], offs[k], o_sem.at[k]) for k in range(n)]
+        for copy in to_scalar:
+            copy.start()
         amount = lax.broadcasted_iota(jnp.int32, (pad, planes), 0)
         for h in range(n // per_hot):
             hot = jnp.concatenate(
                 [jnp.where(picks[k:k + 1, :] == amount, 1.0, 0.0)
                  for k in range(h * per_hot, (h + 1) * per_hot)], axis=0)
             hots[h] = hot.T.astype(jnp.bfloat16)
-        to_scalar.wait()
+        for copy in to_scalar:
+            copy.wait()
 
     done = 0
     for start, end in portions(n):
@@ -312,8 +318,30 @@
     owned, rows, width = cost_out.shape
     pix = width // n
     per_chunk = LANES // pix
-    lane = lax.broadcasted_iota(jnp.int32, (owned + 1, LANES), 1) // pix
     for c in range(width // LANES):
+        at = slice(c * LANES, (c + 1) * LANES)
+        if per_chunk == rows == GROUP:
+            blocks = [pieces[c * rows + k, 0:owned, :] for k in range(rows)]
+            lane = lax.broadcasted_iota(jnp.int32, (owned, LANES), 1) // pix
+            for d in (4, 2, 1):
+                upper = lax.rem(lane // d, 2) == 1
+                for k in range(rows):
+                    if k & d == 0:
+                        a, b = blocks[k], blocks[k + d]
+                        blocks[k] = jnp.where(upper, pltpu.roll(b, d * pix, 1), a)
+                        blocks[k + d] = jnp.where(upper, b, pltpu.roll(a, LANES - d * pix, 1))
+            for r in range(rows):
+                cost_out[:, r, at] = blocks[r]
+            depths = jnp.concatenate([pieces[c * rows + k, owned:, :] for k in range(rows)], axis=0)
+            lane = lax.broadcasted_iota(jnp.int32, (rows, LANES), 1) // pix
+            apart = lane - lax.broadcasted_iota(jnp.int32, (rows, LANES), 0)
+            line = depths
+            for d in range(1, rows):
+                moved = pltpu.roll(pltpu.roll(depths, d * pix, 1), rows - d, 0)
+                line = jnp.where(jnp.logical_or(apart == d, apart == d - rows), moved, line)
+            map_out[:, at] = line
+            continue
+        lane = lax.broadcasted_iota(jnp.int32, (owned + 1, LANES), 1) // pix
         for r in range(rows):
             line = None
             for k in range(per_chunk):
@@ -322,8 +350,8 @@
                 if shift:
                     piece = pltpu.roll(piece, shift, 1)
                 line = piece if line is None else jnp.where(lane == k, piece, line)
-            cost_out[:, r, c * LANES:(c + 1) * LANES] = line[:owned]
-            map_out[r:r + 1, c * LANES:(c + 1) * LANES] = line[owned:]
+            cost_out[:, r, at] = line[:owned]
+            map_out[r:r + 1, at] = line[owned:]
 
 
 def per_device(features, offsets, conf_bins, plane_depths):
@@ -353,9 +381,9 @@
             pltpu.VMEM((n, cg, width), f32),
             pltpu.VMEM((n, 1, planes), jnp.int32),
             pltpu.VMEM((n, 1, planes), f32),
-            pltpu.VMEM((n, planes), jnp.int32),
-            pltpu.SMEM((n, planes), jnp.int32),
-            pltpu.VMEM((n * pad, cg * width // LANES, LANES), f32),
+            pltpu.VMEM((n, 1, planes), jnp.int32),
+            tuple(pltpu.SMEM((1, planes), jnp.int32) for _ in range(n)),
+            pltpu.VMEM((n * pad * cg * width // LANES, LANES), f32),
             pltpu.VMEM((planes, cg * width // LANES, LANES), f32),
             pltpu.VMEM((n, width), f32),
             pltpu.VMEM((n, planes), jnp.int32),
@@ -370,7 +398,7 @@
             pltpu.VMEM((planes, lanes_out), f32),
             pltpu.VMEM((n, owned + 1, lanes_out), f32),
             dma,
-        ] + [dma((n,)) for _ in range(6)] + [dma((groups,))] * 2 + [dma((rows,))] * 2 + [dma((n,))] * 2,
+        ] + [dma((n,)) for _ in range(7)] + [dma((groups,))] * 2 + [dma((rows,))] * 2 + [dma((n,))] * 2,
         compiler_params=pltpu.CompilerParams(collective_id=0, has_side_effects=True,
                                              vmem_limit_bytes=60 << 20),
     )(features, offsets, conf_bins, plane_depths)

time: 33.4 us -> 32.1 us (0.961)
  Pallas kernels: 32.6 us -> 31.2 us
    pallas_call x1, Pallas kernels: 30.7 us -> 29.5 us  [per_device(): pl.pallas_call(functools.partial(kernel, n), out_shape=jax.ShapeDtypeStru...]
where the time goes in v3:
time: 32.1 us; the launch traced here: 31.9 us
  Pallas kernels  31.2 us (97%)
  between operations  0.64 us (2%)
    pallas_call x1, Pallas kernels, per_device(): pl.pallas_call(functools.partial(kernel, n), out_shape=jax.ShapeDtypeStru...  29.5 us
    pallas_call x1, Pallas kernels, per_device(): pl.pallas_call(lay_out, out_shape=(jax.ShapeDtypeStruct((owned, rows, wid...  1.79 us

profile of v3, /device:TPU:0, one launch (start us, length us, event | category | flops | bytes accessed | tf_op | source)
XLA Modules:
  0.0 31.9 jit_solution(16126407859694194089)
XLA Ops:
  0.6 29.5 %shard_map.59.pieces = f32[16,9,128]{2,1,0:T(8,128)} custom-call(f32[1,32,8,256]{3,2,1,0:T(8,128)} %feat_ref.1, s32[1,128]{1,0:T(1,128)} %off_ref.1, s32[8,256]{1,0:T(8,128)} %conf_ref.1, f32[8]{0:T(128)} %depth_ref.1), custom_call_target="tpu_custom_call" | custom-call | tf_op jit(solution)/shard_map/pallas_call | solution.py:373
  30.1 1.8 %shard_map.60 = (f32[8,8,256]{2,1,0:T(8,128)}, f32[8,256]{1,0:T(8,128)}) custom-call(f32[16,9,128]{2,1,0:T(8,128)} %shard_map.59.pieces), custom_call_target="tpu_custom_call" | custom-call | tf_op jit(solution)/shard_map/pallas_call | solution.py:405

commit v4 on v3

--- a/solution.py
+++ b/solution.py
@@ -205,13 +205,16 @@
             for i, source in enumerate(sources):
                 build(k + i, xr[source])
 
-        def receive_two(i, carry):
-            receive(first + 2 * i, 2)
+        batch = min(3, end - first)
+
+        def receive_batch(i, carry):
+            receive(first + batch * i, batch)
             return carry
 
-        lax.fori_loop(0, (end - first) // 2, receive_two, 0)
-        if (end - first) % 2:
-            receive(end - 1, 1)
+        whole = (end - first) // batch
+        lax.fori_loop(0, whole, receive_batch, 0)
+        if (end - first) % batch:
+            receive(first + whole * batch, (end - first) % batch)
         if start == 0:
             take_offsets()
         while (done + 1) * per_hot <= end:
@@ -305,7 +308,7 @@
         feat_copy(me, peer).wait_send()
         return carry
 
-    lax.fori_loop(1, n, finish, 0)
+    each(1, n, lambda k: finish(k, 0))
     each(1, groups, lambda k: half_copy(my_group, lax.rem(my_group + k, groups)).wait_send())
     each(1, rows, lambda k: cost_copy(my_row, lax.rem(my_row + k, rows)).wait_send())
 

time: 32.1 us -> 32 us (level)
  no operation moved by 1% of the time
where the time goes in v4:
time: 32 us; the launch traced here: 31.8 us
  Pallas kernels  31.1 us (97%)
  between operations  0.64 us (2%)
    pallas_call x1, Pallas kernels, per_device(): pl.pallas_call(functools.partial(kernel, n), out_shape=jax.ShapeDtypeStru...  29.3 us
    pallas_call x1, Pallas kernels, per_device(): pl.pallas_call(lay_out, out_shape=(jax.ShapeDtypeStruct((owned, rows, wid...  1.79 us

profile of v4, /device:TPU:0, one launch (start us, length us, event | category | flops | bytes accessed | tf_op | source)
XLA Modules:
  0.0 31.8 jit_solution(4172673909652650380)
XLA Ops:
  0.6 29.3 %shard_map.59.pieces = f32[16,9,128]{2,1,0:T(8,128)} custom-call(f32[1,32,8,256]{3,2,1,0:T(8,128)} %feat_ref.1, s32[1,128]{1,0:T(1,128)} %off_ref.1, s32[8,256]{1,0:T(8,128)} %conf_ref.1, f32[8]{0:T(128)} %depth_ref.1), custom_call_target="tpu_custom_call" | custom-call | tf_op jit(solution)/shard_map/pallas_call | solution.py:376
  30.0 1.8 %shard_map.60 = (f32[8,8,256]{2,1,0:T(8,128)}, f32[8,256]{1,0:T(8,128)}) custom-call(f32[16,9,128]{2,1,0:T(8,128)} %shard_map.59.pieces), custom_call_target="tpu_custom_call" | custom-call | tf_op jit(solution)/shard_map/pallas_call | solution.py:408
